TPU v7x, 32 devices: a whole 2x2x4 slice. The times are simulated.
32 devices in a mesh: row: 8 (over y, x, core), col: 4 (over z).
Axes of the slice: x: 2, y: 2, z: 4, core: 2. Of those that a mesh axis runs over, the one named last changes fastest.
Arguments:
- design: bfloat16 [512, 90112], P(('row', 'col')), may hold values from -6 to 6
- arc_partials: float32 [32, 6, 16], P(('row', 'col')), may hold values from -6 to 6
- arc_id: int32 [32], P(('row', 'col')), may hold values from 0 to 7
- arc_weight: float32 [8], replicated, may hold values from 0.25 to 4
Outputs:
- normal_slab: float32 [90112, 2048], P('row', 'col')
All inputs are finite; a program needn't handle non-finite values.
Results may differ from a plain program's by a relative error of at most 0.0003.
The roundings to bfloat16 on the way count: a program that leaves them out, or rounds other values in their place, can miss the bound.
Values may be sent and summed in bfloat16 or wider, within the bound.
A program may use at most 128 MiB of HBM per device.

v0:
```python
import jax
import jax.numpy as jnp
from jax import lax
from jax.sharding import PartitionSpec as P

SLAB = 2048
ridge = 4.0


def solve_small(matrix, rhs):
    order = matrix.shape[-1]
    for pivot in range(order):
        scale = 1.0 / matrix[..., pivot, pivot]
        row_mat = matrix[..., pivot, :] * scale[..., None]
        row_rhs = rhs[..., pivot, :] * scale[..., None]
        factor = matrix[..., :, pivot]
        matrix = matrix - factor[..., :, None] * row_mat[..., None, :]
        rhs = rhs - factor[..., :, None] * row_rhs[..., None, :]
        matrix = matrix.at[..., pivot, :].set(row_mat)
        rhs = rhs.at[..., pivot, :].set(row_rhs)
    return rhs


def own_reduced(design, arc_partials, arc_id, arc_weight):
    high = lax.Precision.HIGHEST
    slab_rows = design[:, :SLAB].astype(jnp.float32)
    partials = arc_partials[0]
    coupling = jnp.dot(partials, slab_rows, precision=high, preferred_element_type=jnp.float32)
    gram = jnp.dot(partials, partials.T, precision=high, preferred_element_type=jnp.float32)
    arc_count = arc_weight.shape[0]
    select = (jnp.arange(arc_count) == arc_id[0]).astype(jnp.float32)
    arc_gram, arc_coupling = lax.psum(
        (select[:, None, None] * gram[None], select[:, None, None] * coupling[None]), ("row", "col")
    )
    order = partials.shape[0]
    own_gram = jnp.sum(select[:, None, None] * arc_gram, axis=0) + ridge * jnp.eye(
        order, dtype=jnp.float32
    )
    own_coupling = jnp.sum(select[:, None, None] * arc_coupling, axis=0)
    solved = solve_small(own_gram, own_coupling)
    reduced = slab_rows - jnp.dot(
        partials.T, solved, precision=high, preferred_element_type=jnp.float32
    )
    weight = jnp.sum(select * arc_weight)
    return (weight * reduced).astype(jnp.bfloat16)


def make_accumulate(ordered, piece):
    return lax.dot_general(
        piece, ordered, (((0,), (0,)), ((), ())), preferred_element_type=jnp.float32
    )


def col_major(slab_global, row_count, col_count, rows_dev):
    width = slab_global.shape[1]
    ordered = slab_global.reshape(row_count, col_count, rows_dev, width)
    return ordered.transpose(1, 0, 2, 3).reshape(rows_dev * row_count * col_count, width)


def local(design, arc_partials, arc_id, arc_weight):
    rows_dev = design.shape[0]
    row_count = lax.axis_size("row")
    col_count = lax.axis_size("col")
    devices = row_count * col_count
    epochs = rows_dev * devices
    eliminated_own = own_reduced(design, arc_partials, arc_id, arc_weight)
    regrouped = lax.all_to_all(design, "row", split_axis=1, concat_axis=0, tiled=True)
    columns = lax.all_to_all(eliminated_own, "col", split_axis=1, concat_axis=0, tiled=True)
    slab_global = lax.all_gather(columns, "row", axis=0, tiled=True)
    ordered = col_major(slab_global, row_count, col_count, rows_dev)
    normal = make_accumulate(ordered, lax.all_gather(regrouped, "col", axis=0, tiled=True))
    return normal * (1.0 / epochs)


def solution(mesh):
    placed = (P(("row", "col"), None), P(("row", "col"), None, None), P(("row", "col")), P())
    return jax.shard_map(
        local, mesh=mesh, in_specs=placed, out_specs=P("row", "col"), check_vma=False
    )
```

profile of v0, /device:TPU:0, one launch (start us, length us, event | category | flops | bytes accessed | tf_op | source)
XLA Modules:
  0.0 400.1 jit_solution(14108734418693655313)
XLA Ops:
  7.4 3.6 copy.42
  11.0 5.2 %all-to-all-start.1 = ((bf16[16,8,11264]{2,0,1:T(8,128)(2,1)}), bf16[16,8,11264]{2,0,1:T(8,128)(2,1)S(1)}, u32[]{:S(2)}, u32[]{:S(2)}) async-start(bf16[16,8,11264]{2,0,1:T(8,128)(2,1)} %bitcast.64), calls=%async_computation.1 | async-start | bytes 5767168 | tf_op jit(solution)/shard_map/all_to_all | solution.py:67
  16.9 1.0 fusion.3
  17.9 0.8 broadcast_multiply_fusion
  18.8 33.2 %all-to-all-done.1 = bf16[16,8,11264]{2,0,1:T(8,128)(2,1)S(1)} async-done(((bf16[16,8,11264]{2,0,1:T(8,128)(2,1)}), bf16[16,8,11264]{2,0,1:T(8,128)(2,1)S(1)}, u32[]{:S(2)}, u32[]{:S(2)}) %all-to-all-start.1) | async-done | bytes 2883616 | tf_op jit(solution)/shard_map/all_to_all | solution.py:67
  52.0 1.6 copy-done
  53.8 50.2 %psum.15 = f32[8,6,6]{2,0,1:T(8,128)S(1)} all-reduce(f32[8,6,6]{2,0,1:T(8,128)S(1)} %broadcast_multiply_fusion.1), channel_id=1, replica_groups=mesh['row'=8,'col'=4] {'row','col'}, use_global_device_ids=true, to_apply=%region_3.0 | all-reduce | flops 288 | bytes 2304 | tf_op jit(solution)/shard_map/psum | solution.py:32
  104.1 0.5 slice.240
  105.5 0.6 slice.244
  106.8 0.2 slice_reduce_fusion.4
  107.1 0.6 slice.248
  108.4 0.2 slice_reduce_fusion.3
  108.7 0.6 slice.252
  110.0 0.2 slice_reduce_fusion.2
  110.3 0.6 slice.256
  111.5 0.2 slice_reduce_fusion.1
  111.8 0.6 slice.260
  113.2 0.6 fusion.12
  113.8 0.2 slice_reduce_fusion
  114.0 216.3 %all-reduce.2.cloned.1.call-done = f32[8,6,2048]{2,0,1:T(8,128)} async-done(((f32[8,6,2048]{2,0,1:T(8,128)}), f32[8,6,2048]{2,0,1:T(8,128)}) %all-reduce.2.cloned.1.call-update) | async-done | bytes 393232 | tf_op jit(solution)/shard_map/psum | solution.py:32
  330.3 1.2 multiply_reduce_fusion
  331.6 0.2 scatter.36
  331.9 0.2 scatter.40
  332.1 0.2 scatter.44
  332.4 0.2 scatter.46
  332.7 0.2 scatter.50
  333.0 0.2 scatter.54
  333.2 1.7 fusion.2
  334.9 9.2 %all_to_all.38 = bf16[16,4,512]{2,0,1:T(8,128)(2,1)S(1)} all-to-all(bf16[16,4,512]{2,0,1:T(8,128)(2,1)S(1)} %bitcast.70), channel_id=1, replica_groups=mesh['row'=8,'col'=4] {'col'}, dimensions={1} | all-to-all | bytes 131072 | tf_op jit(solution)/shard_map/all_to_all | solution.py:68
  344.1 9.8 %all_gather.6 = bf16[512,512]{1,0:T(8,128)(2,1)S(1)} all-gather(bf16[64,512]{1,0:T(8,128)(2,1)S(1)} %bitcast.69), channel_id=1, replica_groups=mesh['row'=8,'col'=4] {'row'}, dimensions={0}, use_global_device_ids=true | all-gather | bytes 589824 | tf_op jit(solution)/shard_map/all_gather | solution.py:69
  354.0 15.2 %multiply_bitcast_fusion = f32[11264,512]{0,1:T(8,128)} fusion(bf16[512,512]{1,0:T(8,128)(2,1)S(1)} %bitcast.65, bf16[512,11264]{1,0:T(8,128)(2,1)} %all-gather.2.cloned.1.call-done), kind=kOutput, calls=%fused_computation | convolution fusion | flops 5911347200 | bytes 35127296 | tf_op jit(solution)/shard_map/dot_general | solution.py:49
  369.1 23.5 %copy.24 = f32[11264,512]{1,0:T(8,128)} copy(f32[11264,512]{0,1:T(8,128)} %multiply_bitcast_fusion) | data formatting | bytes 46137344 | tf_op jit(solution)/shard_map/mul | solution.py:72
  (50 shorter events, 1.7 us)
Async XLA Ops:
  7.4 9.5 %copy-start.1 = (f32[1,6,16]{2,0,1:T(1,128)S(1)}, f32[1,6,16]{2,0,1:T(1,128)}, u32[]{:S(2)}) copy-start(f32[1,6,16]{2,0,1:T(1,128)} %param.27) | copy-start | bytes 1156
  7.4 105.8 %copy-start.2 = (f32[8]{0:T(128)S(1)}, f32[8]{0:T(128)}, u32[]{:S(2)}) copy-start(f32[8]{0:T(128)} %param.29) | copy-start | bytes 100
  11.0 41.0 %all-to-all-start.1 = ((bf16[16,8,11264]{2,0,1:T(8,128)(2,1)}), bf16[16,8,11264]{2,0,1:T(8,128)(2,1)S(1)}, u32[]{:S(2)}, u32[]{:S(2)}) async-start(bf16[16,8,11264]{2,0,1:T(8,128)(2,1)} %bitcast.64), calls=%async_computation.1 | async-start | bytes 5767168 | tf_op jit(solution)/shard_map/all_to_all | solution.py:67
  16.2 314.1 %all-reduce.2.cloned.1.call-start = ((), (), s32[]{:S(2)}) async-start(), calls=%async_computation.2 | async-start | bytes 786432 | tf_op jit(solution)/shard_map/psum | solution.py:32
  18.8 335.2 %all-gather.2.cloned.1.call-start = ((), (), s32[]{:S(2)}) async-start(), calls=%async_computation.3 | async-start | bytes 14417920 | tf_op jit(solution)/shard_map/all_gather | solution.py:71
  52.0 1.6 copy-start
Sparse Core Ops, SparseCore 0:
  22.3 307.9 all-reduce.1
Sparse Core Ops, SparseCore 1:
  53.7 201.6 all-gather.1
where the time goes:
time: 401 us; the launch traced here: 400 us
  waiting for transfers between devices  250 us (62%)
  blocking collectives  69.1 us (17%)
  local copies, waits for them, and re-layouts  34.6 us (9%)
  between operations  19.7 us (5%)
  matrix products  18 us (4%)
  starting transfers between devices  5.28 us (1%)
    psum x1, waiting for transfers between devices, own_reduced(): lax.psum((select[:, None, None] * gram[None], select[:, None, None] * cou...  216 us
    psum x1, blocking collectives, own_reduced(): lax.psum((select[:, None, None] * gram[None], select[:, None, None] * cou...  50.2 us
    all_to_all x1, waiting for transfers between devices, local(): lax.all_to_all(design, 'row', split_axis=1, concat_axis=0, tiled=True)  33.2 us
    mul x1, local copies, waits for them, and re-layouts, local(): return normal * (1.0 / epochs)  23.5 us
    dot_general x1, matrix products, make_accumulate(): lax.dot_general(piece, ordered, (((0,), (0,)), ((), ())), preferred_eleme...  15.2 us
    all_gather x1, blocking collectives, local(): slab_global = lax.all_gather(columns, 'row', axis=0, tiled=True)  9.79 us
    all_to_all x1, blocking collectives, local(): lax.all_to_all(eliminated_own, 'col', split_axis=1, concat_axis=0, tiled=...  9.18 us
  transfers between devices with their start and end apart: 3, of which 2 were waited for; matrix products, arithmetic and copies ran while one was open for 3% of the time, Pallas kernels for 0%

commit v1 on v0

--- a/solution.py
+++ b/solution.py
@@ -5,6 +5,29 @@
 
 SLAB = 2048
 ridge = 4.0
+
+
+def split_up(shard, dim, size):
+    shape = shard.shape
+    blocks = shard.reshape(*shape[:dim], size, shape[dim] // size, *shape[dim + 1 :])
+    return jnp.moveaxis(blocks, dim, 0)
+
+
+def joined_along(parts, dim):
+    shape = list(parts.shape[1:])
+    shape[dim] *= parts.shape[0]
+    return jnp.moveaxis(parts, 0, dim).reshape(shape)
+
+
+def swapped_with_each(x, axis, split_dim, concat_dim):
+    count, mine = (lax.axis_size(axis), lax.axis_index(axis))
+    pieces = split_up(x, split_dim, count)
+    outs = [pieces[mine]]
+    for step in range(1, count):
+        sent = pieces[mine ^ step]
+        outs.append(lax.ppermute(sent, axis, [(i, i ^ step) for i in range(count)]))
+    pieces = jnp.stack(outs)[mine ^ jnp.arange(count)]
+    return joined_along(pieces, concat_dim)
 
 
 def solve_small(matrix, rhs):
@@ -64,7 +87,7 @@
     devices = row_count * col_count
     epochs = rows_dev * devices
     eliminated_own = own_reduced(design, arc_partials, arc_id, arc_weight)
-    regrouped = lax.all_to_all(design, "row", split_axis=1, concat_axis=0, tiled=True)
+    regrouped = swapped_with_each(design, "row", 1, 0)
     columns = lax.all_to_all(eliminated_own, "col", split_axis=1, concat_axis=0, tiled=True)
     slab_global = lax.all_gather(columns, "row", axis=0, tiled=True)
     ordered = col_major(slab_global, row_count, col_count, rows_dev)

time: 401 us -> 367 us (0.915)
  waiting for transfers between devices: 250 us -> 224 us
  local copies, waits for them, and re-layouts: 34.6 us -> 19.3 us
  starting transfers between devices: 5.28 us -> 9.67 us
    all_to_all x1 -> x0, waiting for transfers between devices: 33.2 us -> none  [local(): lax.all_to_all(design, 'row', split_axis=1, concat_axis=0, tiled=True)]
    ppermute x0 -> x7, waiting for transfers between devices: none -> 26.7 us  [swapped_with_each(): outs.append(lax.ppermute(sent, axis, [(i, i ^ step) for i in range(count)]))]
    mul x1 -> x0, local copies, waits for them, and re-layouts: 23.5 us -> none  [local(): return normal * (1.0 / epochs)]
    psum x1, waiting for transfers between devices: 216 us -> 197 us  [own_reduced(): lax.psum((select[:, None, None] * gram[None], select[:, None, None] * cou...]
    ppermute x0 -> x7, starting transfers between devices: none -> 9.62 us  [swapped_with_each(): outs.append(lax.ppermute(sent, axis, [(i, i ^ step) for i in range(count)]))]
    another operation x0 -> x2, local copies, waits for them, and re-layouts: none -> 6.04 us
    all_to_all x1 -> x0, starting transfers between devices: 5.2 us -> none  [local(): lax.all_to_all(design, 'row', split_axis=1, concat_axis=0, tiled=True)]
  transfers between devices with their start and end apart: 3 -> 9, of which waited for: 2 -> 4; matrix products, arithmetic and copies ran while one was open for 3% -> 6% of each run, Pallas kernels for 0% -> 0%
where the time goes in v1:
time: 367 us; the launch traced here: 366 us
  waiting for transfers between devices  224 us (61%)
  blocking collectives  71.3 us (19%)
  between operations  19.7 us (5%)
  local copies, waits for them, and re-layouts  19.3 us (5%)
  matrix products  18.7 us (5%)
  starting transfers between devices  9.67 us (3%)
  other arithmetic  3.81 us (1%)
    psum x1, waiting for transfers between devices, own_reduced(): lax.psum((select[:, None, None] * gram[None], select[:, None, None] * cou...  197 us
    psum x1, blocking collectives, own_reduced(): lax.psum((select[:, None, None] * gram[None], select[:, None, None] * cou...  52.1 us
    ppermute x7, waiting for transfers between devices, swapped_with_each(): outs.append(lax.ppermute(sent, axis, [(i, i ^ step) for i in range(count)]))  26.7 us
    dot_general x1, matrix products, make_accumulate(): lax.dot_general(piece, ordered, (((0,), (0,)), ((), ())), preferred_eleme...  15.8 us
    all_gather x1, blocking collectives, local(): slab_global = lax.all_gather(columns, 'row', axis=0, tiled=True)  9.97 us
    ppermute x7, starting transfers between devices, swapped_with_each(): outs.append(lax.ppermute(sent, axis, [(i, i ^ step) for i in range(count)]))  9.62 us
    all_to_all x1, blocking collectives, local(): lax.all_to_all(eliminated_own, 'col', split_axis=1, concat_axis=0, tiled=...  9.17 us
  transfers between devices with their start and end apart: 9, of which 4 were waited for; matrix products, arithmetic and copies ran while one was open for 6% of the time, Pallas kernels for 0%

profile of v1, /device:TPU:0, one launch (start us, length us, event | category | flops | bytes accessed | tf_op | source)
XLA Modules:
  0.0 366.1 jit_solution(3693378632902118710)
XLA Ops:
  8.0 1.0 fusion.3
  9.1 0.9 broadcast_multiply_fusion
  10.0 3.4 copy.23
  13.5 6.0 %constant_dynamic-slice_fusion = (bf16[16,1,11264]{2,1,0:T(2,128)(2,1)S(1)}, bf16[16,1,11264]{2,1,0:T(2,128)(2,1)S(1)}, bf16[16,1,11264]{2,1,0:T(2,128)(2,1)S(1)...) fusion(bf16[16,8,11264]{2,1,0:T(8,128)(2,1)S(1)} %bitcast.96, ...), kind=kLoop, calls=%fused_computation.62 | loop fusion | bytes 5767200 | tf_op jit(solution)/shard_map/dynamic-slice.73
  19.6 0.6 collective-permute-start
  20.3 2.6 collective-permute-start.1
  23.3 1.8 collective-permute-start.3
  25.7 2.6 collective-permute-start.5
  28.4 4.1 %collective-permute-done.1 = bf16[16,11264]{1,0:T(8,128)(2,1)S(1)} collective-permute-done((bf16[16,11264]{1,0:T(8,128)(2,1)S(1)}, bf16[16,11264]{1,0:T(8,128)(2,1)S(1)}, u32[]{:S(2)}, u32[]{:S(2)}) %collective-permute-start.1) | collective-permute-done | bytes 360480 | tf_op jit(solution)/shard_map/ppermute | solution.py:28
  32.4 1.8 collective-permute-start.6
  34.3 5.8 %collective-permute-done.2 = bf16[16,11264]{1,0:T(8,128)(2,1)S(1)} collective-permute-done((bf16[16,11264]{1,0:T(8,128)(2,1)S(1)}, bf16[16,11264]{1,0:T(8,128)(2,1)S(1)}, u32[]{:S(2)}, u32[]{:S(2)}) %collective-permute-start.2) | collective-permute-done | bytes 360480 | tf_op jit(solution)/shard_map/ppermute | solution.py:28
  40.2 16.8 %collective-permute-done.4 = bf16[16,11264]{1,0:T(8,128)(2,1)S(1)} collective-permute-done((bf16[16,11264]{1,0:T(8,128)(2,1)S(1)}, bf16[16,11264]{1,0:T(8,128)(2,1)S(1)}, u32[]{:S(2)}, u32[]{:S(2)}) %collective-permute-start.4) | collective-permute-done | bytes 360480 | tf_op jit(solution)/shard_map/ppermute | solution.py:28
  57.1 2.3 gather_fusion
  59.5 0.7 copy-done
  60.3 52.1 %psum.15 = f32[8,6,6]{2,0,1:T(8,128)S(1)} all-reduce(f32[8,6,6]{2,0,1:T(8,128)S(1)} %broadcast_multiply_fusion.1), channel_id=1, replica_groups=mesh['row'=8,'col'=4] {'row','col'}, use_global_device_ids=true, to_apply=%region_3.0 | all-reduce | flops 288 | bytes 2304 | tf_op jit(solution)/shard_map/psum | solution.py:55
  112.5 0.5 slice.240
  113.9 0.6 slice.244
  115.4 0.6 slice.248
  117.1 0.6 slice.252
  118.5 0.6 slice.256
  120.1 0.6 slice.260
  121.3 0.7 fusion.12
  122.1 196.8 %all-reduce.2.cloned.1.call-done = f32[8,6,2048]{2,0,1:T(8,128)} async-done(((f32[8,6,2048]{2,0,1:T(8,128)}), f32[8,6,2048]{2,0,1:T(8,128)}) %all-reduce.2.cloned.1.call-update) | async-done | bytes 393232 | tf_op jit(solution)/shard_map/psum | solution.py:55
  318.9 1.2 multiply_reduce_fusion
  320.2 0.2 scatter.36
  320.5 0.2 scatter.40
  320.8 0.2 scatter.44
  321.1 0.2 scatter.46
  321.8 1.8 fusion.2
  323.7 9.2 %all_to_all.19 = bf16[16,4,512]{2,0,1:T(8,128)(2,1)S(1)} all-to-all(bf16[16,4,512]{2,0,1:T(8,128)(2,1)S(1)} %bitcast.110), channel_id=1, replica_groups=mesh['row'=8,'col'=4] {'col'}, dimensions={1} | all-to-all | bytes 131072 | tf_op jit(solution)/shard_map/all_to_all | solution.py:91
  332.9 10.0 %all_gather.7 = bf16[512,512]{1,0:T(8,128)(2,1)S(1)} all-gather(bf16[64,512]{1,0:T(8,128)(2,1)S(1)} %bitcast.109), channel_id=1, replica_groups=mesh['row'=8,'col'=4] {'row'}, dimensions={0}, use_global_device_ids=true | all-gather | bytes 589824 | tf_op jit(solution)/shard_map/all_gather | solution.py:92
  342.9 15.8 %convolution_multiply_fusion = f32[11264,512]{1,0:T(8,128)} fusion(bf16[512,11264]{1,0:T(8,128)(2,1)} %all-gather.2.cloned.1.call-done, bf16[512,512]{1,0:T(8,128)(2,1)S(1)} %bitcast.100), kind=kOutput, calls=%fused_computation.1 | convolution fusion | flops 5911347200 | bytes 35127296 | tf_op jit(solution)/shard_map/dot_general | solution.py:72
  (78 shorter events, 4.3 us)
Async XLA Ops:
  7.4 311.6 %all-reduce.2.cloned.1.call-start = ((), (), s32[]{:S(2)}) async-start(), calls=%async_computation.2 | async-start | bytes 786432 | tf_op jit(solution)/shard_map/psum | solution.py:55
  9.9 333.0 %all-gather.2.cloned.1.call-start = ((), (), s32[]{:S(2)}) async-start(), calls=%async_computation.1 | async-start | bytes 14417920 | tf_op jit(solution)/shard_map/all_gather | solution.py:94
  19.6 6.1 %collective-permute-start = (bf16[16,11264]{1,0:T(8,128)(2,1)S(1)}, bf16[16,11264]{1,0:T(8,128)(2,1)S(1)}, u32[]{:S(2)}, u32[]{:S(2)}) collective-permute-start(bf16[16,11264]{1,0:T(8,128)(2,1)S(1)} %bitcast.107), channel_id=1, source_target_pairs={{0,4},{4,0},{8,12},{12,8},{16,20},{20,16},{24,28},{28,24},{1,5},{5... | collective-permute-start | bytes 1081352 | tf_op jit(solution)/shard_map/ppermute | solution.py:28
  20.3 12.2 %collective-permute-start.1 = (bf16[16,11264]{1,0:T(8,128)(2,1)S(1)}, bf16[16,11264]{1,0:T(8,128)(2,1)S(1)}, u32[]{:S(2)}, u32[]{:S(2)}) collective-permute-start(bf16[16,11264]{1,0:T(8,128)(2,1)S(1)} %bitcast.106), channel_id=1, source_target_pairs={{0,8},{4,12},{8,0},{12,4},{16,24},{20,28},{24,16},{28,20},{1,9},{5... | collective-permute-start | bytes 1081352 | tf_op jit(solution)/shard_map/ppermute | solution.py:28
  23.0 17.1 %collective-permute-start.2 = (bf16[16,11264]{1,0:T(8,128)(2,1)S(1)}, bf16[16,11264]{1,0:T(8,128)(2,1)S(1)}, u32[]{:S(2)}, u32[]{:S(2)}) collective-permute-start(bf16[16,11264]{1,0:T(8,128)(2,1)S(1)} %bitcast.104), channel_id=1, source_target_pairs={{0,12},{4,8},{8,4},{12,0},{16,28},{20,24},{24,20},{28,16},{1,13},{... | collective-permute-start | bytes 1081352 | tf_op jit(solution)/shard_map/ppermute | solution.py:28
  23.3 16.9 %collective-permute-start.3 = (bf16[16,11264]{1,0:T(8,128)(2,1)S(1)}, bf16[16,11264]{1,0:T(8,128)(2,1)S(1)}, u32[]{:S(2)}, u32[]{:S(2)}) collective-permute-start(bf16[16,11264]{1,0:T(8,128)(2,1)S(1)} %bitcast.103), channel_id=1, source_target_pairs={{0,16},{4,20},{8,24},{12,28},{16,0},{20,4},{24,8},{28,12},{1,17},{... | collective-permute-start | bytes 1081352 | tf_op jit(solution)/shard_map/ppermute | solution.py:28
  25.2 31.8 %collective-permute-start.4 = (bf16[16,11264]{1,0:T(8,128)(2,1)S(1)}, bf16[16,11264]{1,0:T(8,128)(2,1)S(1)}, u32[]{:S(2)}, u32[]{:S(2)}) collective-permute-start(bf16[16,11264]{1,0:T(8,128)(2,1)S(1)} %bitcast.102), channel_id=1, source_target_pairs={{0,20},{4,16},{8,28},{12,24},{16,4},{20,0},{24,12},{28,8},{1,21},{... | collective-permute-start | bytes 1081352 | tf_op jit(solution)/shard_map/ppermute | solution.py:28
  25.7 31.3 %collective-permute-start.5 = (bf16[16,11264]{1,0:T(8,128)(2,1)S(1)}, bf16[16,11264]{1,0:T(8,128)(2,1)S(1)}, u32[]{:S(2)}, u32[]{:S(2)}) collective-permute-start(bf16[16,11264]{1,0:T(8,128)(2,1)S(1)} %bitcast.105), channel_id=1, source_target_pairs={{0,24},{4,28},{8,16},{12,20},{16,8},{20,12},{24,0},{28,4},{1,25},{... | collective-permute-start | bytes 1081352 | tf_op jit(solution)/shard_map/ppermute | solution.py:28
  32.4 24.6 %collective-permute-start.6 = (bf16[16,11264]{1,0:T(8,128)(2,1)S(1)}, bf16[16,11264]{1,0:T(8,128)(2,1)S(1)}, u32[]{:S(2)}, u32[]{:S(2)}) collective-permute-start(bf16[16,11264]{1,0:T(8,128)(2,1)S(1)} %bitcast.101), channel_id=1, source_target_pairs={{0,28},{4,24},{8,20},{12,16},{16,12},{20,8},{24,4},{28,0},{1,29},{... | collective-permute-start | bytes 1081352 | tf_op jit(solution)/shard_map/ppermute | solution.py:28
  59.4 0.7 copy-start
  59.4 61.8 %copy-start.1 = (f32[8]{0:T(128)S(1)}, f32[8]{0:T(128)}, u32[]{:S(2)}) copy-start(f32[8]{0:T(128)} %param.29) | copy-start | bytes 100
Sparse Core Ops, SparseCore 0:
  13.5 305.4 all-reduce.1
Sparse Core Ops, SparseCore 1:
  59.5 204.3 all-gather.1
